TPU v7x, 256 devices: a whole 4x4x8 slice. The times are simulated.
256 devices in a mesh: dom: 16 (over y, x), sub: 16 (over z, core).
Axes of the slice: x: 4, y: 4, z: 8, core: 2. Of those that a mesh axis runs over, the one named last changes fastest.
Arguments:
- coords: float32 [3, 65536], P(None, ('dom', 'sub')), may hold values from -6 to 6
- direction: float32 [3, 65536], P(None, ('dom', 'sub')), may hold values from -6 to 6
- connect: int32 [4, 262144], P(None, ('dom', 'sub')), may hold values from 0 to 383
- shape_inv: float32 [9, 262144], P(None, ('dom', 'sub')), may hold values from -3.5 to 3.5
- weight: float32 [262144], P(('dom', 'sub')), may hold values from 0.3 to 9
- send_node: int32 [256, 128], P(('dom', 'sub')), may hold values from 0 to 255
- recv_slot: int32 [256, 128], P(('dom', 'sub')), may hold values from 0 to 127, each once within a row
Outputs:
- gradient: float32 [4, 3, 65536], P(None, None, ('dom', 'sub'))
- energy: float32 [4], replicated
- min_det: float32 [4], replicated
Inputs may be any that keep to these rules, and one draw needn't show every extreme that they name: `connect`: each tetrahedron's corners are local node numbers: owned nodes below 256, ghost slots above. `send_node`: owned node numbers; a node may be listed several times. `recv_slot`: each row is a permutation of the ghost slots.
All inputs are finite; a program needn't handle non-finite values.
Results may differ from a plain program's by a relative error of at most 0.0001.
Values sent between devices are 32-bit elements; how exact they have to be, the bound alone decides.
A program may use at most 64 MiB of HBM per device.

v0:
```python
import jax
import jax.numpy as jnp
from jax import lax
from jax.sharding import PartitionSpec as P

TRIALS = 4


step_scales = (1.0, 0.5, 0.25, 0.125)


def passed_along(shard, axis, by):
    count = lax.axis_size(axis)
    return lax.ppermute(shard, axis, [(i, (i + by) % count) for i in range(count)])


def jacobian(places, connect, shape_inv):
    elem_count = connect.shape[1]
    corners_all = jnp.take(places, connect.reshape(-1), axis=1).reshape(3, 4, elem_count)
    differ = corners_all[:, 1:] - corners_all[:, :1]
    return [
        [
            differ[row_index, 0] * shape_inv[col_index]
            + differ[row_index, 1] * shape_inv[3 + col_index]
            + differ[row_index, 2] * shape_inv[6 + col_index]
            for col_index in range(3)
        ]
        for row_index in range(3)
    ]


def cofactor(matrix):
    return [
        [
            matrix[1][1] * matrix[2][2] - matrix[1][2] * matrix[2][1],
            matrix[1][2] * matrix[2][0] - matrix[1][0] * matrix[2][2],
            matrix[1][0] * matrix[2][1] - matrix[1][1] * matrix[2][0],
        ],
        [
            matrix[0][2] * matrix[2][1] - matrix[0][1] * matrix[2][2],
            matrix[0][0] * matrix[2][2] - matrix[0][2] * matrix[2][0],
            matrix[0][1] * matrix[2][0] - matrix[0][0] * matrix[2][1],
        ],
        [
            matrix[0][1] * matrix[1][2] - matrix[0][2] * matrix[1][1],
            matrix[0][2] * matrix[1][0] - matrix[0][0] * matrix[1][2],
            matrix[0][0] * matrix[1][1] - matrix[0][1] * matrix[1][0],
        ],
    ]


def element_dets(places, connect, shape_inv):
    matrix = jacobian(places, connect, shape_inv)
    cofac = cofactor(matrix)
    return matrix[0][0] * cofac[0][0] + matrix[0][1] * cofac[0][1] + matrix[0][2] * cofac[0][2]


def barrier_shift(lowest):
    return lowest - 1.0 - jnp.abs(lowest)


def element_grad(places, connect, shape_inv, weight, shift, node_count):
    matrix = jacobian(places, connect, shape_inv)
    cofac = cofactor(matrix)
    determ = matrix[0][0] * cofac[0][0] + matrix[0][1] * cofac[0][1] + matrix[0][2] * cofac[0][2]
    lifted = determ - shift
    squares = matrix[0][0] * matrix[0][0]
    for row_index in range(3):
        for col_index in range(3):
            if row_index + col_index > 0:
                squares = squares + matrix[row_index][col_index] * matrix[row_index][col_index]
    power = lifted ** (-2.0 / 3.0)
    energy_part = jnp.sum(weight * squares * power) / 3.0
    scale_jac = weight * power * (2.0 / 3.0)
    scale_cof = weight * squares * power / lifted * (2.0 / 9.0)
    djac = [
        [
            scale_jac * matrix[row_index][col_index] - scale_cof * cofac[row_index][col_index]
            for col_index in range(3)
        ]
        for row_index in range(3)
    ]
    flat_index = connect.reshape(-1)
    rows_out = []
    for row_index in range(3):
        dedge = [
            djac[row_index][0] * shape_inv[3 * edge_index]
            + djac[row_index][1] * shape_inv[3 * edge_index + 1]
            + djac[row_index][2] * shape_inv[3 * edge_index + 2]
            for edge_index in range(3)
        ]
        rows_out.append(
            jnp.concatenate([-(dedge[0] + dedge[1] + dedge[2]), dedge[0], dedge[1], dedge[2]])
        )
    combined = jnp.stack(rows_out)
    targets = flat_index[None, :] + node_count * jnp.arange(3, dtype=jnp.int32)[:, None]
    summed = jax.ops.segment_sum(
        combined.reshape(-1), targets.reshape(-1), num_segments=3 * node_count
    )
    return (energy_part, summed.reshape(3, node_count))


def global_min(values):
    return lax.pmin(values, ("dom", "sub"))


def global_sum(values):
    return lax.psum(values, ("dom", "sub"))


def send_back(ghost_grads, sends, slots, node_count):
    share_len = sends.shape[0] // 4
    ordered = ghost_grads[..., slots]
    leading = ordered.shape[:-1]
    blocks_all = ordered.reshape(leading + (4, share_len))
    came_all = []
    for block_index, offset in ((0, -1), (1, 1)):
        came_all.append(passed_along(blocks_all[..., block_index, :], "dom", offset))
    for block_index, offset in ((2, -1), (3, 1)):
        came_all.append(passed_along(blocks_all[..., block_index, :], "sub", offset))
    joined = jnp.concatenate(came_all, axis=-1)
    return jnp.zeros(leading + (node_count,), jnp.float32).at[..., sends].add(joined)


def per_device(coords, direction, connect, shape_inv, weight, send_node, recv_slot):
    node_count = coords.shape[1]
    sends = send_node[0]
    slots = recv_slot[0]
    share_len = sends.shape[0] // 4
    both = jnp.concatenate([coords, direction], axis=0)
    outgoing = jnp.take(both, sends, axis=1).reshape(6, 4, share_len)
    arrived = []
    for block_index, offset in ((0, 1), (1, -1)):
        arrived.append(passed_along(outgoing[:, block_index], "dom", offset))
    for block_index, offset in ((2, 1), (3, -1)):
        arrived.append(passed_along(outgoing[:, block_index], "sub", offset))
    arrived_rows = jnp.concatenate(arrived, axis=1)
    ghosts = jnp.zeros_like(arrived_rows).at[:, slots].set(arrived_rows)
    local = jnp.concatenate([both, ghosts], axis=1)
    local_count = local.shape[1]
    local_coords = local[:3]
    local_dir = local[3:]
    elem_total = connect.shape[1] * lax.axis_size("dom") * lax.axis_size("sub")
    lows = []
    totals = []
    grads = []
    for trial_index in range(TRIALS):
        places = local_coords + step_scales[trial_index] * local_dir
        lowest = global_min(jnp.min(element_dets(places, connect, shape_inv)))
        energy_part, grad_rows = element_grad(
            places, connect, shape_inv, weight, barrier_shift(lowest), local_count
        )
        totals.append(global_sum(energy_part))
        owned = grad_rows[:, :node_count] + send_back(
            grad_rows[:, node_count:], sends, slots, node_count
        )
        lows.append(lowest)
        grads.append(owned)
    lowest_all = jnp.stack(lows)
    energy = jnp.stack(totals) / elem_total
    gradient = jnp.stack(grads)
    return (gradient, energy, lowest_all)


def solution(mesh):
    placed = (
        P(None, ("dom", "sub")),
        P(None, ("dom", "sub")),
        P(None, ("dom", "sub")),
        P(None, ("dom", "sub")),
        P(("dom", "sub")),
        P(("dom", "sub"), None),
        P(("dom", "sub"), None),
    )
    return jax.shard_map(
        per_device,
        mesh=mesh,
        in_specs=placed,
        out_specs=(P(None, None, ("dom", "sub")), P(), P()),
        check_vma=False,
    )
```

profile of v0, /device:TPU:1, one launch (start us, length us, event | category | flops | bytes accessed | tf_op | source)
XLA Modules:
  0.0 617.3 jit_solution(7205468279504949322)
XLA Ops:
  3.4 1.3 reduce.3
  4.8 2.1 collective-permute-start
  7.0 3.8 collective-permute-start.1
  10.8 2.5 collective-permute-start.2
  18.9 10.8 %gather_fusion.6 = f32[4096,3]{1,0:T(8,128)S(1)} fusion(f32[3,384]{0,1:T(8,128)S(1)} %get-tuple-element.128, s32[4096]{0:T(1024)S(1)} %fusion.3), kind=kCustom, calls=%fused_computation.1.clone | custom fusion | bytes 114688 | tf_op jit(solution)/shard_map/jit(_take)/gather | solution.py:19
  29.7 14.1 %gather_fusion.7 = f32[4096,3]{1,0:T(8,128)} fusion(f32[3,384]{0,1:T(8,128)S(1)} %get-tuple-element.129, s32[4096]{0:T(1024)S(1)} %fusion.3), kind=kCustom, calls=%fused_computation.2.clone | custom fusion | bytes 114688 | tf_op jit(solution)/shard_map/jit(_take)/gather | solution.py:19
  43.8 14.1 %gather_fusion.8 = f32[4096,3]{1,0:T(8,128)} fusion(f32[3,384]{0,1:T(8,128)S(1)} %get-tuple-element.130, s32[4096]{0:T(1024)S(1)} %fusion.3), kind=kCustom, calls=%fused_computation.3.clone | custom fusion | bytes 114688 | tf_op jit(solution)/shard_map/jit(_take)/gather | solution.py:19
  57.9 14.1 %gather_fusion.5 = f32[4096,3]{1,0:T(8,128)} fusion(f32[3,384]{0,1:T(8,128)S(1)} %get-tuple-element.87, s32[4096]{0:T(1024)S(1)} %fusion.3), kind=kCustom, calls=%fused_computation.clone | custom fusion | bytes 114688 | tf_op jit(solution)/shard_map/jit(_take)/gather | solution.py:19
  71.9 4.5 broadcast_select_fusion.3
  76.5 1.2 slice.273
  78.6 1.3 slice.290
  82.5 2.0 copy.162
  85.9 2.0 copy.169
  89.8 1.3 copy.141
  94.6 77.0 %all-reduce.1 = (f32[]{:T(128)}, f32[]{:T(128)}, f32[]{:T(128)}, f32[]{:T(128)}) all-reduce(f32[]{:T(128)} %get-tuple-element.115, f32[]{:T(128)} %get-tuple-element.102, f32[]{:T(128)} %get-tuple-element.89, f32[]{:T(128)} %get-tuple-element.74), channel_id=1, replica_groups=mesh['dom'=16,'sub'=16] {'dom','sub'}, use_global_device_ids=true, to_apply=%region_14.16 | all-reduce | flops 4 | bytes 32 | tf_op jit(solution)/shard_map/pmin | solution.py:104
  179.1 78.9 %scatter_custom_fusion.1 = f32[1152]{0:T(1024)S(1)} fusion(s32[12288]{0:T(1024)S(1)} %reshape.266, f32[12288]{0:T(1024)S(1)} %reshape.268, f32[]{:T(128)} %constant.19.clone.1), kind=kCustom, calls=%fused_computation.224 | custom fusion | flops 12288 | bytes 4612 | tf_op jit(solution)/shard_map/scatter-add | solution.py:97
  258.2 78.9 %scatter_custom_fusion.3 = f32[1152]{0:T(1024)S(1)} fusion(s32[12288]{0:T(1024)S(1)} %reshape.266, f32[12288]{0:T(1024)S(1)} %reshape.284, f32[]{:T(128)} %constant.19.clone.1), kind=kCustom, calls=%fused_computation.222 | custom fusion | flops 12288 | bytes 4612 | tf_op jit(solution)/shard_map/scatter-add | solution.py:97
  337.2 79.1 %scatter_custom_fusion.5 = f32[1152]{0:T(1024)S(1)} fusion(s32[12288]{0:T(1024)S(1)} %reshape.266, f32[12288]{0:T(1024)S(1)} %reshape.300, f32[]{:T(128)} %constant.19.clone.1), kind=kCustom, calls=%fused_computation.220 | custom fusion | flops 12288 | bytes 4612 | tf_op jit(solution)/shard_map/scatter-add | solution.py:97
  417.2 78.9 %scatter_custom_fusion.7 = f32[1152]{0:T(1024)S(1)} fusion(s32[12288]{0:T(1024)S(1)} %reshape.266, f32[12288]{0:T(1024)S(1)} %reshape.316, f32[]{:T(128)} %constant.19.clone.1), kind=kCustom, calls=%fused_computation.218 | custom fusion | flops 12288 | bytes 4612 | tf_op jit(solution)/shard_map/scatter-add | solution.py:97
  499.5 2.2 collective-permute-start.4
  502.4 1.4 collective-permute-start.7
  507.4 3.1 pad_maximum_fusion.19
  510.5 79.5 %all-reduce = (f32[1]{0:T(128)}, f32[1]{0:T(128)}, f32[1]{0:T(128)}, f32[1]{0:T(128)}) all-reduce(f32[1]{0:T(128)} %bitcast.119, f32[1]{0:T(128)} %bitcast.118, f32[1]{0:T(128)} %bitcast.117, f32[1]{0:T(128)} %bitcast.116), channel_id=1, replica_groups=mesh['dom'=16,'sub'=16] {'dom','sub'}, use_global_device_ids=true, to_apply=%region_24.26 | all-reduce | flops 4 | bytes 32 | tf_op jit(solution)/shard_map/psum | solution.py:108
  590.0 3.0 maximum_multiply_fusion
  593.5 1.4 collective-permute-start.11
  596.4 4.5 collective-permute-start.12
  601.2 1.6 collective-permute-start.15
  602.8 4.8 collective-permute-start.16
  607.7 1.3 scatter_fusion
  611.2 1.3 scatter_fusion.1
  612.7 1.3 scatter_fusion.2
  615.3 1.3 scatter_fusion.3
  (168 shorter events, 33.7 us)
Async XLA Ops:
  4.8 12.7 %collective-permute-start = (f32[6,32]{1,0:T(8,128)S(1)}, f32[6,32]{1,0:T(8,128)S(1)}, u32[]{:S(2)}, u32[]{:S(2)}) collective-permute-start(f32[6,32]{1,0:T(8,128)S(1)} %get-tuple-element.260), channel_id=1, source_target_pairs={{0,16},{16,32},{32,48},{48,64},{64,80},{80,96},{96,112},{112,128},... | collective-permute-start | bytes 2312 | tf_op jit(solution)/shard_map/ppermute | solution.py:14
  7.0 10.6 %collective-permute-start.1 = (f32[6,32]{1,0:T(8,128)S(1)}, f32[6,32]{1,0:T(8,128)S(1)}, u32[]{:S(2)}, u32[]{:S(2)}) collective-permute-start(f32[6,32]{1,0:T(8,128)S(1)} %get-tuple-element.263), channel_id=1, source_target_pairs={{0,240},{16,0},{32,16},{48,32},{64,48},{80,64},{96,80},{112,96},{1... | collective-permute-start | bytes 2312 | tf_op jit(solution)/shard_map/ppermute | solution.py:14
  10.8 6.8 %collective-permute-start.2 = (f32[6,32]{1,0:T(8,128)S(1)}, f32[6,32]{1,0:T(8,128)S(1)}, u32[]{:S(2)}, u32[]{:S(2)}) collective-permute-start(f32[6,32]{1,0:T(8,128)S(1)} %get-tuple-element.262), channel_id=1, source_target_pairs={{0,1},{1,2},{2,3},{3,4},{4,5},{5,6},{6,7},{7,8},{8,9},{9,10},{10,1... | collective-permute-start | bytes 2312 | tf_op jit(solution)/shard_map/ppermute | solution.py:14
  13.3 4.3 collective-permute-start.3
  89.8 2.0 copy-start
  89.8 86.9 %copy-start.1 = (f32[1024]{0:T(1024)S(1)}, f32[1024]{0:T(1024)}, u32[]{:S(2)}) copy-start(f32[1024]{0:T(1024)} %param.13) | copy-start | bytes 12292
  499.5 94.0 %collective-permute-start.4 = (f32[3,32]{1,0:T(4,128)S(1)}, f32[3,32]{1,0:T(4,128)S(1)}, u32[]{:S(2)}, u32[]{:S(2)}) collective-permute-start(f32[3,32]{1,0:T(4,128)S(1)} %bitcast.309), channel_id=1, source_target_pairs={{0,240},{16,0},{32,16},{48,32},{64,48},{80,64},{96,80},{112,96},{1... | collective-permute-start | bytes 1160 | tf_op jit(solution)/shard_map/ppermute | solution.py:14
  501.8 93.1 %collective-permute-start.5 = (f32[3,32]{1,0:T(4,128)S(1)}, f32[3,32]{1,0:T(4,128)S(1)}, u32[]{:S(2)}, u32[]{:S(2)}) collective-permute-start(f32[3,32]{1,0:T(4,128)S(1)} %bitcast.307), channel_id=1, source_target_pairs={{0,16},{16,32},{32,48},{48,64},{64,80},{80,96},{96,112},{112,128},... | collective-permute-start | bytes 1160 | tf_op jit(solution)/shard_map/ppermute | solution.py:14
  501.8 94.2 %collective-permute-start.6 = (f32[3,32]{1,0:T(4,128)S(1)}, f32[3,32]{1,0:T(4,128)S(1)}, u32[]{:S(2)}, u32[]{:S(2)}) collective-permute-start(f32[3,32]{1,0:T(4,128)S(1)} %bitcast.306), channel_id=1, source_target_pairs={{0,15},{1,0},{2,1},{3,2},{4,3},{5,4},{6,5},{7,6},{8,7},{9,8},{10,9... | collective-permute-start | bytes 1160 | tf_op jit(solution)/shard_map/ppermute | solution.py:14
  502.4 93.9 %collective-permute-start.7 = (f32[3,32]{1,0:T(4,128)S(1)}, f32[3,32]{1,0:T(4,128)S(1)}, u32[]{:S(2)}, u32[]{:S(2)}) collective-permute-start(f32[3,32]{1,0:T(4,128)S(1)} %bitcast.305), channel_id=1, source_target_pairs={{0,1},{1,2},{2,3},{3,4},{4,5},{5,6},{6,7},{7,8},{8,9},{9,10},{10,1... | collective-permute-start | bytes 1160 | tf_op jit(solution)/shard_map/ppermute | solution.py:14
  504.8 96.1 %collective-permute-start.10 = (f32[3,32]{1,0:T(4,128)S(1)}, f32[3,32]{1,0:T(4,128)S(1)}, u32[]{:S(2)}, u32[]{:S(2)}) collective-permute-start(f32[3,32]{1,0:T(4,128)S(1)} %bitcast.310), channel_id=1, source_target_pairs={{0,15},{1,0},{2,1},{3,2},{4,3},{5,4},{6,5},{7,6},{8,7},{9,8},{10,9... | collective-permute-start | bytes 1160 | tf_op jit(solution)/shard_map/ppermute | solution.py:14
  593.5 7.5 %collective-permute-start.11 = (f32[3,32]{1,0:T(4,128)S(1)}, f32[3,32]{1,0:T(4,128)S(1)}, u32[]{:S(2)}, u32[]{:S(2)}) collective-permute-start(f32[3,32]{1,0:T(4,128)S(1)} %bitcast.308), channel_id=1, source_target_pairs={{0,1},{1,2},{2,3},{3,4},{4,5},{5,6},{6,7},{7,8},{8,9},{9,10},{10,1... | collective-permute-start | bytes 1160 | tf_op jit(solution)/shard_map/ppermute | solution.py:14
  594.9 6.3 %collective-permute-start.8 = (f32[3,32]{1,0:T(4,128)S(1)}, f32[3,32]{1,0:T(4,128)S(1)}, u32[]{:S(2)}, u32[]{:S(2)}) collective-permute-start(f32[3,32]{1,0:T(4,128)S(1)} %bitcast.304), channel_id=1, source_target_pairs={{0,240},{16,0},{32,16},{48,32},{64,48},{80,64},{96,80},{112,96},{1... | collective-permute-start | bytes 1160 | tf_op jit(solution)/shard_map/ppermute | solution.py:14
  596.1 6.7 %collective-permute-start.9 = (f32[3,32]{1,0:T(4,128)S(1)}, f32[3,32]{1,0:T(4,128)S(1)}, u32[]{:S(2)}, u32[]{:S(2)}) collective-permute-start(f32[3,32]{1,0:T(4,128)S(1)} %bitcast.303), channel_id=1, source_target_pairs={{0,16},{16,32},{32,48},{48,64},{64,80},{80,96},{96,112},{112,128},... | collective-permute-start | bytes 1160 | tf_op jit(solution)/shard_map/ppermute | solution.py:14
  596.4 12.9 %collective-permute-start.12 = (f32[3,32]{1,0:T(4,128)S(1)}, f32[3,32]{1,0:T(4,128)S(1)}, u32[]{:S(2)}, u32[]{:S(2)}) collective-permute-start(f32[3,32]{1,0:T(4,128)S(1)} %bitcast.302), channel_id=1, source_target_pairs={{0,240},{16,0},{32,16},{48,32},{64,48},{80,64},{96,80},{112,96},{1... | collective-permute-start | bytes 1160 | tf_op jit(solution)/shard_map/ppermute | solution.py:14
  601.0 8.4 %collective-permute-start.13 = (f32[3,32]{1,0:T(4,128)S(1)}, f32[3,32]{1,0:T(4,128)S(1)}, u32[]{:S(2)}, u32[]{:S(2)}) collective-permute-start(f32[3,32]{1,0:T(4,128)S(1)} %bitcast.300), channel_id=1, source_target_pairs={{0,16},{16,32},{32,48},{48,64},{64,80},{80,96},{96,112},{112,128},... | collective-permute-start | bytes 1160 | tf_op jit(solution)/shard_map/ppermute | solution.py:14
  601.0 9.2 %collective-permute-start.14 = (f32[3,32]{1,0:T(4,128)S(1)}, f32[3,32]{1,0:T(4,128)S(1)}, u32[]{:S(2)}, u32[]{:S(2)}) collective-permute-start(f32[3,32]{1,0:T(4,128)S(1)} %bitcast.297), channel_id=1, source_target_pairs={{0,15},{1,0},{2,1},{3,2},{4,3},{5,4},{6,5},{7,6},{8,7},{9,8},{10,9... | collective-permute-start | bytes 1160 | tf_op jit(solution)/shard_map/ppermute | solution.py:14
  601.2 9.9 %collective-permute-start.15 = (f32[3,32]{1,0:T(4,128)S(1)}, f32[3,32]{1,0:T(4,128)S(1)}, u32[]{:S(2)}, u32[]{:S(2)}) collective-permute-start(f32[3,32]{1,0:T(4,128)S(1)} %bitcast.296), channel_id=1, source_target_pairs={{0,1},{1,2},{2,3},{3,4},{4,5},{5,6},{6,7},{7,8},{8,9},{9,10},{10,1... | collective-permute-start | bytes 1160 | tf_op jit(solution)/shard_map/ppermute | solution.py:14
  602.8 11.3 %collective-permute-start.16 = (f32[3,32]{1,0:T(4,128)S(1)}, f32[3,32]{1,0:T(4,128)S(1)}, u32[]{:S(2)}, u32[]{:S(2)}) collective-permute-start(f32[3,32]{1,0:T(4,128)S(1)} %bitcast.295), channel_id=1, source_target_pairs={{0,240},{16,0},{32,16},{48,32},{64,48},{80,64},{96,80},{112,96},{1... | collective-permute-start | bytes 1160 | tf_op jit(solution)/shard_map/ppermute | solution.py:14
  609.2 5.8 collective-permute-start.17
  609.3 5.7 collective-permute-start.18
  610.2 4.9 collective-permute-start.19
where the time goes:
time: 619 us; the launch traced here: 617 us
  other arithmetic  344 us (56%)
  blocking collectives  157 us (25%)
  local copies, waits for them, and re-layouts  78.6 us (13%)
  starting transfers between devices  28.6 us (5%)
  between operations  8.91 us (1%)
    scatter-add x4, other arithmetic, element_grad(): jax.ops.segment_sum(combined.reshape(-1), targets.reshape(-1), num_segmen...  316 us
    psum x1, blocking collectives, global_sum(): return lax.psum(values, ('dom', 'sub'))  79.5 us
    pmin x1, blocking collectives, global_min(): return lax.pmin(values, ('dom', 'sub'))  77 us
    gather x4, local copies, waits for them, and re-layouts, jacobian(): jnp.take(places, connect.reshape(-1), axis=1).reshape(3, 4, elem_count)  53 us
    ppermute x20, starting transfers between devices, passed_along(): lax.ppermute(shard, axis, [(i, (i + by) % count) for i in range(count)])  28.6 us
  transfers between devices with their start and end apart: 20, of which 1 were waited for; matrix products, arithmetic and copies ran while one was open for 3% of the time, Pallas kernels for 0%

commit v1 on v0

v1 whole, which is shorter than its diff:
```python
import functools

import jax
import jax.numpy as jnp
from jax import lax
from jax.experimental import pallas as pl
from jax.experimental.pallas import tpu as pltpu
from jax.sharding import PartitionSpec as P

TRIALS = 4
LANES = 128
ROWS = 16
MESH = pl.DeviceIdType.MESH
step_scales = (1.0, 0.5, 0.25, 0.125)


def far_first(count):
    return sorted(range(1, count), key=lambda j: -min(j, count - j))


def take_lanes(table, index):
    return jnp.take_along_axis(table, index, axis=1, mode="promise_in_bounds")


def cofactor(m):
    return [
        [
            m[1][1] * m[2][2] - m[1][2] * m[2][1],
            m[1][2] * m[2][0] - m[1][0] * m[2][2],
            m[1][0] * m[2][1] - m[1][1] * m[2][0],
        ],
        [
            m[0][2] * m[2][1] - m[0][1] * m[2][2],
            m[0][0] * m[2][2] - m[0][2] * m[2][0],
            m[0][1] * m[2][0] - m[0][0] * m[2][1],
        ],
        [
            m[0][1] * m[1][2] - m[0][2] * m[1][1],
            m[0][2] * m[1][0] - m[0][0] * m[1][2],
            m[0][0] * m[1][1] - m[0][1] * m[1][0],
        ],
    ]


def split3(x):
    high = x.astype(jnp.bfloat16)
    rest = x - high.astype(jnp.float32)
    mid = rest.astype(jnp.bfloat16)
    low = (rest - mid.astype(jnp.float32)).astype(jnp.bfloat16)
    return jnp.concatenate([high, mid, low], axis=0)


def dot_nt(a, b):
    return lax.dot_general(a, b, (((1,), (1,)), ((), ())), preferred_element_type=jnp.float32)


def fold3(acc):
    return acc[:ROWS] + acc[ROWS : 2 * ROWS] + acc[2 * ROWS :]


def pack(values, op):
    lane = lax.broadcasted_iota(jnp.int32, (8, LANES), 1)
    half = [op(v, pltpu.roll(v, 64, 1)) for v in values]
    first = jnp.where(lane < 64, half[0], half[1])
    second = jnp.where(lane < 64, half[2], half[3])
    first = op(first, pltpu.roll(first, 32, 1))
    second = op(second, pltpu.roll(second, 96, 1))
    return jnp.where((lane // 32) % 2 == 1, first, second)


def unpack_mask():
    lane = lax.broadcasted_iota(jnp.int32, (8, LANES), 1)
    row = lax.broadcasted_iota(jnp.int32, (8, LANES), 0)
    group = lane // 32
    trial = jnp.where(group == 0, 2, jnp.where(group == 1, 0, jnp.where(group == 2, 3, 1)))
    return trial == row


def kernel(
    nd,
    ns,
    coords,
    direction,
    connect,
    shape_inv,
    weight,
    send_node,
    recv_slot,
    grad_ref,
    stat_ref,
    co_v,
    di_v,
    con_v,
    inv_v,
    w_v,
    snd_v,
    rcv_v,
    out_tile,
    halo,
    idx_v,
    onehot,
    back_hot,
    cmat,
    gtile,
    gback,
    rows_v,
    sub_min,
    dom_min,
    sub_sum,
    dom_sum,
    in_sem,
    halo_send,
    halo_recv,
    back_send,
    back_recv,
    sub_sems,
    dom_sems,
):
    f32 = jnp.float32
    d = lax.axis_index("dom")
    s = lax.axis_index("sub")
    nodes = co_v.shape[1]
    local = onehot.shape[0]
    chunks = con_v.shape[0] * 8

    loads = [
        pltpu.make_async_copy(coords, co_v, in_sem.at[0]),
        pltpu.make_async_copy(direction, di_v, in_sem.at[1]),
        pltpu.make_async_copy(send_node, snd_v, in_sem.at[2]),
        pltpu.make_async_copy(recv_slot, rcv_v, in_sem.at[3]),
        pltpu.make_async_copy(weight, w_v, in_sem.at[4]),
    ]
    wide = []
    for k in range(8):
        cut = pl.ds(k * LANES, LANES)
        wide.append(pltpu.make_async_copy(connect.at[:, cut], con_v.at[:, k, :], in_sem.at[5 + k]))
        wide.append(pltpu.make_async_copy(shape_inv.at[:, cut], inv_v.at[:, k, :], in_sem.at[13 + k]))
    for copy in loads + wide:
        copy.start()

    barrier = pltpu.get_barrier_semaphore()
    for j in far_first(ns):
        pl.semaphore_signal(barrier, inc=1, device_id=(d, lax.rem(s + j, ns)), device_id_type=MESH)
    for j in far_first(nd):
        pl.semaphore_signal(barrier, inc=1, device_id=(lax.rem(d + j, nd), s), device_id_type=MESH)

    lane = lax.broadcasted_iota(jnp.int32, (8, LANES), 1)
    block = lane // 32
    for copy in loads:
        copy.wait()

    send_idx = jnp.broadcast_to(snd_v[...], (8, LANES))
    pad = jnp.zeros((2, nodes), f32)
    both = jnp.concatenate([co_v[...], di_v[...], pad], axis=0)
    picked = take_lanes(both[:, :LANES], send_idx & 127)
    for k in range(1, nodes // LANES):
        part = take_lanes(both[:, k * LANES : (k + 1) * LANES], send_idx & 127)
        picked = jnp.where(send_idx >= k * LANES, part, picked)
    out_tile[...] = picked

    pl.semaphore_wait(barrier, nd - 1 + ns - 1)

    ahead = (
        (lax.rem(d + 1, nd), s),
        (lax.rem(d + nd - 1, nd), s),
        (d, lax.rem(s + 1, ns)),
        (d, lax.rem(s + ns - 1, ns)),
    )
    behind = (ahead[1], ahead[0], ahead[3], ahead[2])
    shares = [
        pltpu.make_async_remote_copy(
            src_ref=out_tile,
            dst_ref=halo.at[k],
            send_sem=halo_send.at[k],
            recv_sem=halo_recv.at[k],
            device_id=ahead[k],
            device_id_type=MESH,
        )
        for k in range(4)
    ]
    for copy in shares:
        copy.start()

    for copy in wide:
        copy.wait()

    slot_row = jnp.broadcast_to(rcv_v[...], (LANES, LANES))
    slot_hot = jnp.where(slot_row == lax.broadcasted_iota(jnp.int32, (LANES, LANES), 0), 1.0, 0.0).astype(jnp.bfloat16)
    arrival = dot_nt(lane.astype(f32).astype(jnp.bfloat16), slot_hot).astype(jnp.int32)
    corner = []
    for c in range(4):
        idx = con_v[c]
        ghost = idx >= nodes
        idx = jnp.where(ghost, nodes + take_lanes(arrival, jnp.where(ghost, idx - nodes, 0)), idx)
        idx_v[pl.ds(8 * c, 8), :] = idx
        corner.append(idx)

    owned = []
    for q in range(6):
        source = (co_v if q < 3 else di_v)
        r = q % 3
        per = []
        for c in range(4):
            low = corner[c] & 127
            value = take_lanes(jnp.broadcast_to(source[r : r + 1, :LANES], (8, LANES)), low)
            for k in range(1, nodes // LANES):
                part = take_lanes(
                    jnp.broadcast_to(source[r : r + 1, k * LANES : (k + 1) * LANES], (8, LANES)), low
                )
                value = jnp.where(corner[c] >= k * LANES, part, value)
            per.append(value)
        owned.append(per)

    send_row = jnp.broadcast_to(snd_v[...], (nodes, LANES))
    back_hot[...] = jnp.where(
        send_row == lax.broadcasted_iota(jnp.int32, (nodes, LANES), 0), 1.0, 0.0
    ).astype(jnp.bfloat16)

    for copy in shares:
        copy.wait_recv()
    came = halo[0]
    for k in range(1, 4):
        came = jnp.where(block == k, halo[k], came)

    values = []
    for q in range(6):
        row = jnp.broadcast_to(came[q : q + 1, :], (8, LANES))
        values.append(
            [jnp.where(corner[c] >= nodes, take_lanes(row, corner[c] & 127), owned[q][c]) for c in range(4)]
        )
    w9 = [inv_v[i] for i in range(9)]

    def edges_times_inverse(base):
        out = []
        for r in range(3):
            edge = [values[base + r][c] - values[base + r][0] for c in (1, 2, 3)]
            out.append([edge[0] * w9[m] + edge[1] * w9[3 + m] + edge[2] * w9[6 + m] for m in range(3)])
        return out

    jac_x = edges_times_inverse(0)
    jac_d = edges_times_inverse(3)
    jacs = []
    cofs = []
    dets = []
    for t in range(TRIALS):
        a = step_scales[t]
        m = [[jac_x[r][k] + a * jac_d[r][k] for k in range(3)] for r in range(3)]
        cof = cofactor(m)
        jacs.append(m)
        cofs.append(cof)
        dets.append(m[0][0] * cof[0][0] + m[0][1] * cof[0][1] + m[0][2] * cof[0][2])

    def start_stage(row, buf, sems, axis):
        me, count = (s, ns) if axis == "sub" else (d, nd)
        copies = []
        for j in far_first(count):
            peer = lax.rem(me + j, count)
            copies.append(
                pltpu.make_async_remote_copy(
                    src_ref=row,
                    dst_ref=buf.at[pl.ds(me, 1), :],
                    send_sem=sems.at[0, j - 1],
                    recv_sem=sems.at[1, j - 1],
                    device_id=(d, peer) if axis == "sub" else (peer, s),
                    device_id_type=MESH,
                )
            )
        for copy in copies:
            copy.start()
        return copies

    def finish_stage(row, buf, copies, axis, reduce):
        me, count = (s, ns) if axis == "sub" else (d, nd)
        for copy in copies:
            copy.wait_recv()
        mine = lax.broadcasted_iota(jnp.int32, (count, LANES), 0) == me
        return reduce(jnp.where(mine, row, buf[...]), axis=0, keepdims=True)

    def build_hot(first, last):
        node = lax.broadcasted_iota(jnp.int32, (local, LANES), 0)

        def step(j, carry):
            row = jnp.broadcast_to(idx_v[pl.ds(j, 1), :], (local, LANES))
            onehot[:, pl.ds(pl.multiple_of(j * LANES, LANES), LANES)] = jnp.where(row == node, 1.0, 0.0).astype(
                jnp.bfloat16
            )
            return carry

        lax.fori_loop(first, last, step, 0)

    row = jnp.min(pack(dets, jnp.minimum), axis=0, keepdims=True)
    rows_v[0] = row
    flights = start_stage(rows_v.at[0], sub_min, sub_sems.at[0], "sub")
    sends = list(flights)
    weights = w_v[...]
    squares = []
    for t in range(TRIALS):
        total = jacs[t][0][0] * jacs[t][0][0]
        for r in range(3):
            for k in range(3):
                if r + k > 0:
                    total = total + jacs[t][r][k] * jacs[t][r][k]
        squares.append(weights * total)
    build_hot(0, chunks // 2)
    row = finish_stage(row, sub_min, flights, "sub", jnp.min)
    rows_v[1] = row
    flights = start_stage(rows_v.at[1], dom_min, dom_sems.at[0], "dom")
    sends += flights
    build_hot(chunks // 2, chunks)
    row = finish_stage(row, dom_min, flights, "dom", jnp.min)

    mask = unpack_mask()
    lowest = jnp.min(jnp.where(mask, jnp.broadcast_to(row, (8, LANES)), jnp.inf), axis=1, keepdims=True)
    shift = lowest - 1.0 - jnp.abs(lowest)

    energies = []
    scale_jac = []
    scale_cof = []
    for t in range(TRIALS):
        lifted = dets[t] - jnp.broadcast_to(shift[t : t + 1, :], (8, LANES))
        power = jnp.exp(jnp.log(lifted) * (-2.0 / 3.0))
        energy = squares[t] * power
        energies.append(energy)
        scale_jac.append(weights * power * (2.0 / 3.0))
        scale_cof.append(energy / lifted * (2.0 / 9.0))

    row = jnp.sum(pack(energies, jnp.add), axis=0, keepdims=True)
    rows_v[2] = row
    flights = start_stage(rows_v.at[2], sub_sum, sub_sems.at[1], "sub")
    sends += flights

    for t in range(TRIALS):
        for r in range(3):
            g = [scale_jac[t] * jacs[t][r][k] - scale_cof[t] * cofs[t][r][k] for k in range(3)]
            h = [g[0] * w9[3 * e] + g[1] * w9[3 * e + 1] + g[2] * w9[3 * e + 2] for e in range(3)]
            h = [-(h[0] + h[1] + h[2])] + h
            for c in range(4):
                cmat[pl.ds(8 * ROWS * c + 3 * t + r, 8, stride=ROWS), :] = h[c]

    def scatter_step(j, acc):
        pair = [split3(cmat[pl.ds(pl.multiple_of((2 * j + i) * ROWS, ROWS), ROWS), :]) for i in range(2)]
        left = jnp.concatenate(pair, axis=1)
        right = onehot[:, pl.ds(pl.multiple_of(j * 2 * LANES, LANES), 2 * LANES)]
        return acc + dot_nt(left, right)

    summed = fold3(lax.fori_loop(0, chunks // 2, scatter_step, jnp.zeros((3 * ROWS, local), f32)))
    gtile[...] = summed[:, nodes:]
    returns = [
        pltpu.make_async_remote_copy(
            src_ref=gtile,
            dst_ref=gback.at[k],
            send_sem=back_send.at[k],
            recv_sem=back_recv.at[k],
            device_id=behind[k],
            device_id_type=MESH,
        )
        for k in range(4)
    ]
    for copy in returns:
        copy.start()

    row = finish_stage(row, sub_sum, flights, "sub", jnp.sum)
    rows_v[3] = row
    flights = start_stage(rows_v.at[3], dom_sum, dom_sems.at[1], "dom")
    sends += flights

    for copy in returns:
        copy.wait_recv()
    wide_block = lax.broadcasted_iota(jnp.int32, (ROWS, LANES), 1) // 32
    came = gback[0]
    for k in range(1, 4):
        came = jnp.where(wide_block == k, gback[k], came)
    total = summed[:, :nodes] + fold3(dot_nt(split3(came), back_hot[...]))
    for t in range(TRIALS):
        grad_ref[t] = total[3 * t : 3 * t + 3, :]

    row = finish_stage(row, dom_sum, flights, "dom", jnp.sum)
    energy = jnp.sum(jnp.where(mask, jnp.broadcast_to(row, (8, LANES)), 0.0), axis=1, keepdims=True)
    energy = energy / 3.0 / (nd * ns * chunks // 4 * LANES)
    diagonal = lane == lax.broadcasted_iota(jnp.int32, (8, LANES), 0)
    stat_ref[0:1, :] = jnp.sum(jnp.where(diagonal, energy, 0.0), axis=0, keepdims=True)
    stat_ref[1:2, :] = jnp.sum(jnp.where(diagonal, jnp.where(lowest < jnp.inf, lowest, 0.0), 0.0), axis=0, keepdims=True)

    for copy in shares + sends + returns:
        copy.wait_send()


def per_device(nd, ns, coords, direction, connect, shape_inv, weight, send_node, recv_slot):
    f32 = jnp.float32
    nodes = coords.shape[1]
    ghosts = send_node.shape[1]
    local = nodes + ghosts
    elems = connect.shape[1]
    per_row = elems // LANES
    chunks = 4 * per_row
    dma = pltpu.SemaphoreType.DMA
    any_space = pl.BlockSpec(memory_space=pl.ANY)
    vmem = pl.BlockSpec(memory_space=pltpu.VMEM)
    gradient, stats = pl.pallas_call(
        functools.partial(kernel, nd, ns),
        out_shape=(
            jax.ShapeDtypeStruct((TRIALS, 3, nodes), f32),
            jax.ShapeDtypeStruct((2, LANES), f32),
        ),
        in_specs=[any_space] * 7,
        out_specs=(vmem, vmem),
        scratch_shapes=[
            pltpu.VMEM((3, nodes), f32),
            pltpu.VMEM((3, nodes), f32),
            pltpu.VMEM((4, per_row, LANES), jnp.int32),
            pltpu.VMEM((9, per_row, LANES), f32),
            pltpu.VMEM((per_row, LANES), f32),
            pltpu.VMEM((1, ghosts), jnp.int32),
            pltpu.VMEM((1, ghosts), jnp.int32),
            pltpu.VMEM((8, ghosts), f32),
            pltpu.VMEM((4, 8, ghosts), f32),
            pltpu.VMEM((chunks, LANES), jnp.int32),
            pltpu.VMEM((local, 4 * elems), jnp.bfloat16),
            pltpu.VMEM((nodes, ghosts), jnp.bfloat16),
            pltpu.VMEM((chunks * ROWS, LANES), f32),
            pltpu.VMEM((ROWS, ghosts), f32),
            pltpu.VMEM((4, ROWS, ghosts), f32),
            pltpu.VMEM((4, 1, LANES), f32),
            pltpu.VMEM((ns, LANES), f32),
            pltpu.VMEM((nd, LANES), f32),
            pltpu.VMEM((ns, LANES), f32),
            pltpu.VMEM((nd, LANES), f32),
            dma((21,)),
            dma((4,)),
            dma((4,)),
            dma((4,)),
            dma((4,)),
            dma((2, 2, ns - 1)),
            dma((2, 2, nd - 1)),
        ],
        compiler_params=pltpu.CompilerParams(collective_id=0, has_side_effects=True),
        name="trial_energy",
    )(coords, direction, connect, shape_inv, weight.reshape(per_row, LANES), send_node, recv_slot)
    return gradient, stats[0, :TRIALS], stats[1, :TRIALS]


def solution(mesh):
    placed = (
        P(None, ("dom", "sub")),
        P(None, ("dom", "sub")),
        P(None, ("dom", "sub")),
        P(None, ("dom", "sub")),
        P(("dom", "sub")),
        P(("dom", "sub"), None),
        P(("dom", "sub"), None),
    )
    return jax.shard_map(
        functools.partial(per_device, mesh.shape["dom"], mesh.shape["sub"]),
        mesh=mesh,
        in_specs=placed,
        out_specs=(P(None, None, ("dom", "sub")), P(), P()),
        check_vma=False,
    )
```

time: 619 us -> 37.7 us (0.06)
  other arithmetic: 344 us -> 0 us
  blocking collectives: 157 us -> 0 us
  local copies, waits for them, and re-layouts: 78.6 us -> 1.84 us
  Pallas kernels: 0 us -> 35.1 us
  starting transfers between devices: 28.6 us -> 0 us
  between operations: 8.91 us -> 0.65 us
    scatter-add x8 -> x0, other arithmetic: 321 us -> none  [the longest x4 316 us: element_grad(): jax.ops.segment_sum(combined.reshape(-1), targets.reshape(-1), num_segmen...]
    psum x1 -> x0, blocking collectives: 79.5 us -> none  [global_sum(): return lax.psum(values, ('dom', 'sub'))]
    pmin x1 -> x0, blocking collectives: 77 us -> none  [global_min(): return lax.pmin(values, ('dom', 'sub'))]
    gather x10 -> x0, local copies, waits for them, and re-layouts: 56.4 us -> none  [the longest x4 53 us: jacobian(): jnp.take(places, connect.reshape(-1), axis=1).reshape(3, 4, elem_count)]
    pallas_call x0 -> x1, Pallas kernels: none -> 35.1 us  [per_device(): pl.pallas_call(functools.partial(kernel, nd, ns), out_shape=(jax.ShapeDty...]
    ppermute x20 -> x0, starting transfers between devices: 28.6 us -> none  [passed_along(): lax.ppermute(shard, axis, [(i, (i + by) % count) for i in range(count)])]
    unnamed x34 -> x3, local copies, waits for them, and re-layouts: 8.8 us -> 1.32 us
    sub x8 -> x0, local copies, waits for them, and re-layouts: 7.31 us -> none  [jacobian(): differ = corners_all[:, 1:] - corners_all[:, :1]]
  transfers between devices with their start and end apart: 20 -> 0, of which waited for: 1 -> 0; matrix products, arithmetic and copies ran while one was open for 3% -> 0% of each run, Pallas kernels for 0% -> 0%
where the time goes in v1:
time: 37.7 us; the launch traced here: 37.6 us
  Pallas kernels  35.1 us (93%)
  local copies, waits for them, and re-layouts  1.84 us (5%)
  between operations  0.65 us (2%)
    pallas_call x1, Pallas kernels, per_device(): pl.pallas_call(functools.partial(kernel, nd, ns), out_shape=(jax.ShapeDty...  35.1 us
    unnamed x3, local copies, waits for them, and re-layouts  1.32 us

profile of v1, /device:TPU:1, one launch (start us, length us, event | category | flops | bytes accessed | tf_op | source)
XLA Modules:
  0.0 37.6 jit_solution(484498289869218179)
XLA Ops:
  0.6 35.1 %trial_energy.1 = (f32[4,3,256]{2,1,0:T(4,128)}, f32[2,128]{1,0:T(2,128)}) custom-call(f32[3,256]{1,0:T(4,128)} %coords.1, f32[3,256]{1,0:T(4,128)} %direction.1, s32[4,1024]{1,0:T(4,128)} %connect.1, f32[9,1024]{1,0:T(8,128)} %shape_inv.1, f32[8,128]{1,0:T(8,128)} %bitcast.5, s32[1,128]{1,0:T(1,128)} %send_node.1, s32[1,128]{1,0:T(1,128)} %recv_slot.1), custom_call_target="tpu_custom_call" | custom-call | tf_op jit(solution)/shard_map/trial_energy/pallas_call | solution.py:399
  35.7 0.0 copy-start
  35.7 1.3 %copy.10 = f32[4,3,256]{2,0,1:T(4,128)} copy(f32[4,3,256]{2,1,0:T(4,128)} %get-tuple-element.7) | data formatting | bytes 24576
  37.0 0.0 copy-done
  37.0 0.5 %slice_bitcast_fusion = (f32[4]{0:T(128)}, f32[4]{0:T(128)}) fusion(f32[2,128]{1,0:T(2,128)S(1)} %copy-done), kind=kLoop, calls=%fused_computation | loop fusion | bytes 64 | tf_op jit(solution)/shard_map/squeeze | solution.py:439
Async XLA Ops:
  35.7 1.3 %copy-start = (f32[2,128]{1,0:T(2,128)S(1)}, f32[2,128]{1,0:T(2,128)}, u32[]{:S(2)}) copy-start(f32[2,128]{1,0:T(2,128)} %get-tuple-element.6) | copy-start | bytes 3076

commit v2 on v1

--- a/solution.py
+++ b/solution.py
@@ -14,8 +14,12 @@
 step_scales = (1.0, 0.5, 0.25, 0.125)
 
 
-def far_first(count):
-    return sorted(range(1, count), key=lambda j: -min(j, count - j))
+def far_first(count, width=1):
+    def far(j):
+        x, y = j % width, j // width
+        return min(x, width - x) + min(y, count // width - y)
+
+    return sorted(range(1, count), key=lambda j: -far(j))
 
 
 def take_lanes(table, index):
@@ -115,6 +119,7 @@
     back_recv,
     sub_sems,
     dom_sems,
+    known,
 ):
     f32 = jnp.float32
     d = lax.axis_index("dom")
@@ -135,18 +140,20 @@
         cut = pl.ds(k * LANES, LANES)
         wide.append(pltpu.make_async_copy(connect.at[:, cut], con_v.at[:, k, :], in_sem.at[5 + k]))
         wide.append(pltpu.make_async_copy(shape_inv.at[:, cut], inv_v.at[:, k, :], in_sem.at[13 + k]))
-    for copy in loads + wide:
+    for copy in loads[:3]:
         copy.start()
 
     barrier = pltpu.get_barrier_semaphore()
-    for j in far_first(ns):
+    for j in far_first(nd, 4):
+        pl.semaphore_signal(barrier, inc=1, device_id=(lax.rem(d + j, nd), s), device_id_type=MESH)
+    for j in (1, ns - 1):
         pl.semaphore_signal(barrier, inc=1, device_id=(d, lax.rem(s + j, ns)), device_id_type=MESH)
-    for j in far_first(nd):
-        pl.semaphore_signal(barrier, inc=1, device_id=(lax.rem(d + j, nd), s), device_id_type=MESH)
+    for copy in loads[3:] + wide:
+        copy.start()
 
     lane = lax.broadcasted_iota(jnp.int32, (8, LANES), 1)
     block = lane // 32
-    for copy in loads:
+    for copy in loads[:3]:
         copy.wait()
 
     send_idx = jnp.broadcast_to(snd_v[...], (8, LANES))
@@ -158,7 +165,7 @@
         picked = jnp.where(send_idx >= k * LANES, part, picked)
     out_tile[...] = picked
 
-    pl.semaphore_wait(barrier, nd - 1 + ns - 1)
+    pl.semaphore_wait(barrier, nd - 1 + 2)
 
     ahead = (
         (lax.rem(d + 1, nd), s),
@@ -181,7 +188,7 @@
     for copy in shares:
         copy.start()
 
-    for copy in wide:
+    for copy in loads[3:] + wide:
         copy.wait()
 
     slot_row = jnp.broadcast_to(rcv_v[...], (LANES, LANES))
@@ -218,6 +225,18 @@
 
     for copy in shares:
         copy.wait_recv()
+    reach = 2
+    hops = []
+    while reach < ns // 2:
+        hops.append(reach)
+        reach *= 2
+
+    def greet(i):
+        for j in (hops[i], ns - hops[i]):
+            pl.semaphore_signal(known.at[i], inc=1, device_id=(d, lax.rem(s + j, ns)), device_id_type=MESH)
+
+    if hops:
+        greet(0)
     came = halo[0]
     for k in range(1, 4):
         came = jnp.where(block == k, halo[k], came)
@@ -253,7 +272,7 @@
     def start_stage(row, buf, sems, axis):
         me, count = (s, ns) if axis == "sub" else (d, nd)
         copies = []
-        for j in far_first(count):
+        for j in far_first(count, 1 if axis == "sub" else 4):
             peer = lax.rem(me + j, count)
             copies.append(
                 pltpu.make_async_remote_copy(
@@ -290,7 +309,7 @@
 
     row = jnp.min(pack(dets, jnp.minimum), axis=0, keepdims=True)
     rows_v[0] = row
-    flights = start_stage(rows_v.at[0], sub_min, sub_sems.at[0], "sub")
+    flights = start_stage(rows_v.at[0], dom_min, dom_sems.at[0], "dom")
     sends = list(flights)
     weights = w_v[...]
     squares = []
@@ -302,12 +321,16 @@
                     total = total + jacs[t][r][k] * jacs[t][r][k]
         squares.append(weights * total)
     build_hot(0, chunks // 2)
-    row = finish_stage(row, sub_min, flights, "sub", jnp.min)
+    for i in range(len(hops)):
+        pl.semaphore_wait(known.at[i], 2)
+        if i + 1 < len(hops):
+            greet(i + 1)
+    row = finish_stage(row, dom_min, flights, "dom", jnp.min)
     rows_v[1] = row
-    flights = start_stage(rows_v.at[1], dom_min, dom_sems.at[0], "dom")
+    flights = start_stage(rows_v.at[1], sub_min, sub_sems.at[0], "sub")
     sends += flights
     build_hot(chunks // 2, chunks)
-    row = finish_stage(row, dom_min, flights, "dom", jnp.min)
+    row = finish_stage(row, sub_min, flights, "sub", jnp.min)
 
     mask = unpack_mask()
     lowest = jnp.min(jnp.where(mask, jnp.broadcast_to(row, (8, LANES)), jnp.inf), axis=1, keepdims=True)
@@ -335,7 +358,7 @@
             h = [g[0] * w9[3 * e] + g[1] * w9[3 * e + 1] + g[2] * w9[3 * e + 2] for e in range(3)]
             h = [-(h[0] + h[1] + h[2])] + h
             for c in range(4):
-                cmat[pl.ds(8 * ROWS * c + 3 * t + r, 8, stride=ROWS), :] = h[c]
+                cmat[pl.ds(8 * ROWS * c + TRIALS * r + t, 8, stride=ROWS), :] = h[c]
 
     def scatter_step(j, acc):
         pair = [split3(cmat[pl.ds(pl.multiple_of((2 * j + i) * ROWS, ROWS), ROWS), :]) for i in range(2)]
@@ -371,8 +394,8 @@
     for k in range(1, 4):
         came = jnp.where(wide_block == k, gback[k], came)
     total = summed[:, :nodes] + fold3(dot_nt(split3(came), back_hot[...]))
-    for t in range(TRIALS):
-        grad_ref[t] = total[3 * t : 3 * t + 3, :]
+    for r in range(3):
+        grad_ref[r] = total[TRIALS * r : TRIALS * r + TRIALS, :]
 
     row = finish_stage(row, dom_sum, flights, "dom", jnp.sum)
     energy = jnp.sum(jnp.where(mask, jnp.broadcast_to(row, (8, LANES)), 0.0), axis=1, keepdims=True)
@@ -396,10 +419,11 @@
     dma = pltpu.SemaphoreType.DMA
     any_space = pl.BlockSpec(memory_space=pl.ANY)
     vmem = pl.BlockSpec(memory_space=pltpu.VMEM)
+    operands = (coords, direction, connect, shape_inv, weight.reshape(per_row, LANES), send_node, recv_slot)
     gradient, stats = pl.pallas_call(
         functools.partial(kernel, nd, ns),
         out_shape=(
-            jax.ShapeDtypeStruct((TRIALS, 3, nodes), f32),
+            jax.ShapeDtypeStruct((3, TRIALS, nodes), f32),
             jax.ShapeDtypeStruct((2, LANES), f32),
         ),
         in_specs=[any_space] * 7,
@@ -432,11 +456,14 @@
             dma((4,)),
             dma((2, 2, ns - 1)),
             dma((2, 2, nd - 1)),
+            pltpu.SemaphoreType.REGULAR((4,)),
         ],
-        compiler_params=pltpu.CompilerParams(collective_id=0, has_side_effects=True),
+        compiler_params=pltpu.CompilerParams(
+            collective_id=0, has_side_effects=True, vmem_limit_bytes=1 << 24
+        ),
         name="trial_energy",
-    )(coords, direction, connect, shape_inv, weight.reshape(per_row, LANES), send_node, recv_slot)
-    return gradient, stats[0, :TRIALS], stats[1, :TRIALS]
+    )(*(pltpu.with_memory_space_constraint(x, pltpu.HBM) for x in operands))
+    return gradient.transpose(1, 0, 2), stats[0, :TRIALS], stats[1, :TRIALS]
 
 
 def solution(mesh):

time: 37.7 us -> 34.6 us (0.918)
  Pallas kernels: 35.1 us -> 32.7 us
  local copies, waits for them, and re-layouts: 1.84 us -> 1.12 us
    pallas_call x1, Pallas kernels: 35.1 us -> 32.7 us  [per_device(): pl.pallas_call(functools.partial(kernel, nd, ns), out_shape=(jax.ShapeDty...]
    unnamed x3 -> x1, local copies, waits for them, and re-layouts: 1.32 us -> 0.6 us
where the time goes in v2:
time: 34.6 us; the launch traced here: 34.5 us
  Pallas kernels  32.7 us (95%)
  local copies, waits for them, and re-layouts  1.12 us (3%)
  between operations  0.64 us (2%)
    pallas_call x1, Pallas kernels, per_device(): pl.pallas_call(functools.partial(kernel, nd, ns), out_shape=(jax.ShapeDty...  32.7 us

profile of v2, /device:TPU:1, one launch (start us, length us, event | category | flops | bytes accessed | tf_op | source)
XLA Modules:
  0.0 34.5 jit_solution(9264272846556345766)
XLA Ops:
  0.6 32.7 %trial_energy.1 = (f32[3,4,256]{2,1,0:T(4,128)S(1)}, f32[2,128]{1,0:T(2,128)S(1)}) custom-call(f32[3,256]{1,0:T(4,128)} %coords.1, f32[3,256]{1,0:T(4,128)} %direction.1, s32[4,1024]{1,0:T(4,128)} %connect.1, f32[9,1024]{1,0:T(8,128)} %shape_inv.1, f32[8,128]{1,0:T(8,128)} %bitcast.7, s32[1,128]{1,0:T(1,128)} %send_node.1, s32[1,128]{1,0:T(1,128)} %recv_slot.1), custom_call_target="tpu_custom_call" | custom-call | tf_op jit(solution)/shard_map/trial_energy/pallas_call | solution.py:423
  33.4 0.5 %slice_bitcast_fusion = (f32[4]{0:T(128)}, f32[4]{0:T(128)}) fusion(f32[2,128]{1,0:T(2,128)S(1)} %get-tuple-element.6), kind=kLoop, calls=%fused_computation | loop fusion | bytes 64 | tf_op jit(solution)/shard_map/squeeze | solution.py:466
  33.9 0.6 %copy.11 = f32[4,3,256]{2,0,1:T(4,128)} copy(f32[4,3,256]{2,0,1:T(4,128)S(1)} %bitcast.6) | data formatting | bytes 24576

commit v3 on v2

--- a/solution.py
+++ b/solution.py
@@ -91,7 +91,8 @@
     send_node,
     recv_slot,
     grad_ref,
-    stat_ref,
+    energy_ref,
+    lowest_ref,
     co_v,
     di_v,
     con_v,
@@ -397,15 +398,30 @@
     for r in range(3):
         grad_ref[r] = total[TRIALS * r : TRIALS * r + TRIALS, :]
 
+    diagonal = lane == lax.broadcasted_iota(jnp.int32, (8, LANES), 0)
+
+    def along_lanes(column):
+        return jnp.sum(jnp.where(diagonal, column, 0.0), axis=0, keepdims=True)
+
+    finite = jnp.where(lax.broadcasted_iota(jnp.int32, (8, 1), 0) < TRIALS, lowest, 0.0)
+    lowest_ref[...] = along_lanes(finite)[0, :TRIALS]
+    for copy in shares + sends + returns:
+        copy.wait_send()
+
     row = finish_stage(row, dom_sum, flights, "dom", jnp.sum)
     energy = jnp.sum(jnp.where(mask, jnp.broadcast_to(row, (8, LANES)), 0.0), axis=1, keepdims=True)
     energy = energy / 3.0 / (nd * ns * chunks // 4 * LANES)
-    diagonal = lane == lax.broadcasted_iota(jnp.int32, (8, LANES), 0)
-    stat_ref[0:1, :] = jnp.sum(jnp.where(diagonal, energy, 0.0), axis=0, keepdims=True)
-    stat_ref[1:2, :] = jnp.sum(jnp.where(diagonal, jnp.where(lowest < jnp.inf, lowest, 0.0), 0.0), axis=0, keepdims=True)
-
-    for copy in shares + sends + returns:
-        copy.wait_send()
+    energy_ref[...] = along_lanes(energy)[0, :TRIALS]
+
+
+def copy_out(*refs):
+    half = len(refs) // 2
+    sems = refs[-1]
+    copies = [pltpu.make_async_copy(refs[i], refs[half + i], sems.at[i]) for i in range(half)]
+    for copy in copies:
+        copy.start()
+    for copy in copies:
+        copy.wait()
 
 
 def per_device(nd, ns, coords, direction, connect, shape_inv, weight, send_node, recv_slot):
@@ -420,14 +436,16 @@
     any_space = pl.BlockSpec(memory_space=pl.ANY)
     vmem = pl.BlockSpec(memory_space=pltpu.VMEM)
     operands = (coords, direction, connect, shape_inv, weight.reshape(per_row, LANES), send_node, recv_slot)
-    gradient, stats = pl.pallas_call(
+    results = (
+        jax.ShapeDtypeStruct((3, TRIALS, nodes), f32),
+        jax.ShapeDtypeStruct((TRIALS,), f32),
+        jax.ShapeDtypeStruct((TRIALS,), f32),
+    )
+    held = pl.pallas_call(
         functools.partial(kernel, nd, ns),
-        out_shape=(
-            jax.ShapeDtypeStruct((3, TRIALS, nodes), f32),
-            jax.ShapeDtypeStruct((2, LANES), f32),
-        ),
+        out_shape=results,
         in_specs=[any_space] * 7,
-        out_specs=(vmem, vmem),
+        out_specs=(vmem,) * 3,
         scratch_shapes=[
             pltpu.VMEM((3, nodes), f32),
             pltpu.VMEM((3, nodes), f32),
@@ -441,7 +459,7 @@
             pltpu.VMEM((chunks, LANES), jnp.int32),
             pltpu.VMEM((local, 4 * elems), jnp.bfloat16),
             pltpu.VMEM((nodes, ghosts), jnp.bfloat16),
-            pltpu.VMEM((chunks * ROWS, LANES), f32),
+            pltpu.VMEM(((chunks + 1) * ROWS, LANES), f32),
             pltpu.VMEM((ROWS, ghosts), f32),
             pltpu.VMEM((4, ROWS, ghosts), f32),
             pltpu.VMEM((4, 1, LANES), f32),
@@ -463,7 +481,16 @@
         ),
         name="trial_energy",
     )(*(pltpu.with_memory_space_constraint(x, pltpu.HBM) for x in operands))
-    return gradient.transpose(1, 0, 2), stats[0, :TRIALS], stats[1, :TRIALS]
+    gradient, energy, lowest = pl.pallas_call(
+        copy_out,
+        out_shape=results,
+        in_specs=[vmem] * 3,
+        out_specs=(any_space,) * 3,
+        scratch_shapes=[dma((3,))],
+        compiler_params=pltpu.CompilerParams(vmem_limit_bytes=1 << 20),
+        name="copy_out",
+    )(*held)
+    return gradient.transpose(1, 0, 2), energy, lowest
 
 
 def solution(mesh):

time: 34.6 us -> 34 us (0.983)
  local copies, waits for them, and re-layouts: 1.12 us -> 0 us
  Pallas kernels: 32.7 us -> 33.2 us
    unnamed x1 -> x0, local copies, waits for them, and re-layouts: 0.6 us -> none
    pallas_call x1 -> x2, Pallas kernels: 32.7 us -> 33.2 us  [the longest x1 32.6 us: per_device(): pl.pallas_call(functools.partial(kernel, nd, ns), out_shape=results, in_s...]
    squeeze x1 -> x0, local copies, waits for them, and re-layouts: 0.52 us -> none  [per_device(): return (gradient.transpose(1, 0, 2), stats[0, :TRIALS], stats[1, :TRIALS])]
where the time goes in v3:
time: 34 us; the launch traced here: 33.9 us
  Pallas kernels  33.2 us (98%)
  between operations  0.64 us (2%)
    pallas_call x1, Pallas kernels, per_device(): pl.pallas_call(functools.partial(kernel, nd, ns), out_shape=results, in_s...  32.6 us

profile of v3, /device:TPU:1, one launch (start us, length us, event | category | flops | bytes accessed | tf_op | source)
XLA Modules:
  0.0 33.9 jit_solution(13741660142145330428)
XLA Ops:
  0.6 32.6 %trial_energy.1 = (f32[3,4,256]{2,1,0:T(4,128)S(1)}, f32[4]{0:T(128)S(1)}, f32[4]{0:T(128)S(1)}) custom-call(f32[3,256]{1,0:T(4,128)} %coords.1, f32[3,256]{1,0:T(4,128)} %direction.1, s32[4,1024]{1,0:T(4,128)} %connect.1, f32[9,1024]{1,0:T(8,128)} %shape_inv.1, f32[8,128]{1,0:T(8,128)} %bitcast.2, s32[1,128]{1,0:T(1,128)} %send_node.1, s32[1,128]{1,0:T(1,128)} %recv_slot.1), custom_call_target="tpu_custom_call" | custom-call | tf_op jit(solution)/shard_map/trial_energy/pallas_call | solution.py:444
  33.2 0.6 %copy_out.1 = (f32[3,4,256]{2,1,0:T(4,128)}, f32[4]{0:T(128)}, f32[4]{0:T(128)}) custom-call(f32[3,4,256]{2,1,0:T(4,128)S(1)} %get-tuple-element.9.refs_0_, f32[4]{0:T(128)S(1)} %get-tuple-element.10.refs_1_, f32[4]{0:T(128)S(1)} %get-tuple-element.11.refs_2_), custom_call_target="tpu_custom_call" | custom-call | tf_op jit(solution)/shard_map/copy_out/pallas_call | solution.py:484

commit v4 on v3

--- a/solution.py
+++ b/solution.py
@@ -60,6 +60,10 @@
 
 def fold3(acc):
     return acc[:ROWS] + acc[ROWS : 2 * ROWS] + acc[2 * ROWS :]
+
+
+def wait_all(like, sem):
+    pltpu.make_async_copy(like, like, sem).wait()
 
 
 def pack(values, op):
@@ -114,10 +118,8 @@
     sub_sum,
     dom_sum,
     in_sem,
-    halo_send,
-    halo_recv,
-    back_send,
-    back_recv,
+    halo_sems,
+    back_sems,
     sub_sems,
     dom_sems,
     known,
@@ -139,8 +141,8 @@
     wide = []
     for k in range(8):
         cut = pl.ds(k * LANES, LANES)
-        wide.append(pltpu.make_async_copy(connect.at[:, cut], con_v.at[:, k, :], in_sem.at[5 + k]))
-        wide.append(pltpu.make_async_copy(shape_inv.at[:, cut], inv_v.at[:, k, :], in_sem.at[13 + k]))
+        wide.append(pltpu.make_async_copy(connect.at[:, cut], con_v.at[:, k, :], in_sem.at[5]))
+        wide.append(pltpu.make_async_copy(shape_inv.at[:, cut], inv_v.at[:, k, :], in_sem.at[6]))
     for copy in loads[:3]:
         copy.start()
 
@@ -179,8 +181,8 @@
         pltpu.make_async_remote_copy(
             src_ref=out_tile,
             dst_ref=halo.at[k],
-            send_sem=halo_send.at[k],
-            recv_sem=halo_recv.at[k],
+            send_sem=halo_sems.at[0],
+            recv_sem=halo_sems.at[1],
             device_id=ahead[k],
             device_id_type=MESH,
         )
@@ -189,8 +191,10 @@
     for copy in shares:
         copy.start()
 
-    for copy in loads[3:] + wide:
+    for copy in loads[3:]:
         copy.wait()
+    wait_all(con_v, in_sem.at[5])
+    wait_all(inv_v, in_sem.at[6])
 
     slot_row = jnp.broadcast_to(rcv_v[...], (LANES, LANES))
     slot_hot = jnp.where(slot_row == lax.broadcasted_iota(jnp.int32, (LANES, LANES), 0), 1.0, 0.0).astype(jnp.bfloat16)
@@ -224,8 +228,7 @@
         send_row == lax.broadcasted_iota(jnp.int32, (nodes, LANES), 0), 1.0, 0.0
     ).astype(jnp.bfloat16)
 
-    for copy in shares:
-        copy.wait_recv()
+    wait_all(halo, halo_sems.at[1])
     reach = 2
     hops = []
     while reach < ns // 2:
@@ -279,20 +282,18 @@
                 pltpu.make_async_remote_copy(
                     src_ref=row,
                     dst_ref=buf.at[pl.ds(me, 1), :],
-                    send_sem=sems.at[0, j - 1],
-                    recv_sem=sems.at[1, j - 1],
+                    send_sem=sems.at[0],
+                    recv_sem=sems.at[1],
                     device_id=(d, peer) if axis == "sub" else (peer, s),
                     device_id_type=MESH,
                 )
             )
         for copy in copies:
             copy.start()
-        return copies
-
-    def finish_stage(row, buf, copies, axis, reduce):
+
+    def finish_stage(row, buf, sems, axis, reduce):
         me, count = (s, ns) if axis == "sub" else (d, nd)
-        for copy in copies:
-            copy.wait_recv()
+        wait_all(buf.at[pl.ds(0, count - 1), :], sems.at[1])
         mine = lax.broadcasted_iota(jnp.int32, (count, LANES), 0) == me
         return reduce(jnp.where(mine, row, buf[...]), axis=0, keepdims=True)
 
@@ -310,8 +311,7 @@
 
     row = jnp.min(pack(dets, jnp.minimum), axis=0, keepdims=True)
     rows_v[0] = row
-    flights = start_stage(rows_v.at[0], dom_min, dom_sems.at[0], "dom")
-    sends = list(flights)
+    start_stage(rows_v.at[0], dom_min, dom_sems.at[0], "dom")
     weights = w_v[...]
     squares = []
     for t in range(TRIALS):
@@ -326,12 +326,11 @@
         pl.semaphore_wait(known.at[i], 2)
         if i + 1 < len(hops):
             greet(i + 1)
-    row = finish_stage(row, dom_min, flights, "dom", jnp.min)
+    row = finish_stage(row, dom_min, dom_sems.at[0], "dom", jnp.min)
     rows_v[1] = row
-    flights = start_stage(rows_v.at[1], sub_min, sub_sems.at[0], "sub")
-    sends += flights
+    start_stage(rows_v.at[1], sub_min, sub_sems.at[0], "sub")
     build_hot(chunks // 2, chunks)
-    row = finish_stage(row, sub_min, flights, "sub", jnp.min)
+    row = finish_stage(row, sub_min, sub_sems.at[0], "sub", jnp.min)
 
     mask = unpack_mask()
     lowest = jnp.min(jnp.where(mask, jnp.broadcast_to(row, (8, LANES)), jnp.inf), axis=1, keepdims=True)
@@ -350,8 +349,7 @@
 
     row = jnp.sum(pack(energies, jnp.add), axis=0, keepdims=True)
     rows_v[2] = row
-    flights = start_stage(rows_v.at[2], sub_sum, sub_sems.at[1], "sub")
-    sends += flights
+    start_stage(rows_v.at[2], sub_sum, sub_sems.at[1], "sub")
 
     for t in range(TRIALS):
         for r in range(3):
@@ -373,8 +371,8 @@
         pltpu.make_async_remote_copy(
             src_ref=gtile,
             dst_ref=gback.at[k],
-            send_sem=back_send.at[k],
-            recv_sem=back_recv.at[k],
+            send_sem=back_sems.at[0],
+            recv_sem=back_sems.at[1],
             device_id=behind[k],
             device_id_type=MESH,
         )
@@ -383,13 +381,11 @@
     for copy in returns:
         copy.start()
 
-    row = finish_stage(row, sub_sum, flights, "sub", jnp.sum)
+    row = finish_stage(row, sub_sum, sub_sems.at[1], "sub", jnp.sum)
     rows_v[3] = row
-    flights = start_stage(rows_v.at[3], dom_sum, dom_sems.at[1], "dom")
-    sends += flights
-
-    for copy in returns:
-        copy.wait_recv()
+    start_stage(rows_v.at[3], dom_sum, dom_sems.at[1], "dom")
+
+    wait_all(gback, back_sems.at[1])
     wide_block = lax.broadcasted_iota(jnp.int32, (ROWS, LANES), 1) // 32
     came = gback[0]
     for k in range(1, 4):
@@ -405,10 +401,13 @@
 
     finite = jnp.where(lax.broadcasted_iota(jnp.int32, (8, 1), 0) < TRIALS, lowest, 0.0)
     lowest_ref[...] = along_lanes(finite)[0, :TRIALS]
-    for copy in shares + sends + returns:
-        copy.wait_send()
-
-    row = finish_stage(row, dom_sum, flights, "dom", jnp.sum)
+    wait_all(halo, halo_sems.at[0])
+    wait_all(gback, back_sems.at[0])
+    for i in range(2):
+        wait_all(sub_min.at[pl.ds(0, ns - 1), :], sub_sems.at[i, 0])
+        wait_all(dom_min.at[pl.ds(0, nd - 1), :], dom_sems.at[i, 0])
+
+    row = finish_stage(row, dom_sum, dom_sems.at[1], "dom", jnp.sum)
     energy = jnp.sum(jnp.where(mask, jnp.broadcast_to(row, (8, LANES)), 0.0), axis=1, keepdims=True)
     energy = energy / 3.0 / (nd * ns * chunks // 4 * LANES)
     energy_ref[...] = along_lanes(energy)[0, :TRIALS]
@@ -467,14 +466,12 @@
             pltpu.VMEM((nd, LANES), f32),
             pltpu.VMEM((ns, LANES), f32),
             pltpu.VMEM((nd, LANES), f32),
-            dma((21,)),
-            dma((4,)),
-            dma((4,)),
-            dma((4,)),
-            dma((4,)),
-            dma((2, 2, ns - 1)),
-            dma((2, 2, nd - 1)),
-            pltpu.SemaphoreType.REGULAR((4,)),
+            dma((7,)),
+            dma((2,)),
+            dma((2,)),
+            dma((2, 2)),
+            dma((2, 2)),
+            pltpu.SemaphoreType.REGULAR((2,)),
         ],
         compiler_params=pltpu.CompilerParams(
             collective_id=0, has_side_effects=True, vmem_limit_bytes=1 << 24

time: 34 us -> 32.7 us (0.962)
  Pallas kernels: 33.2 us -> 31.9 us
    pallas_call x1, Pallas kernels: 32.6 us -> 31.3 us  [per_device(): pl.pallas_call(functools.partial(kernel, nd, ns), out_shape=results, in_s...]
where the time goes in v4:
time: 32.7 us; the launch traced here: 32.5 us
  Pallas kernels  31.9 us (98%)
  between operations  0.64 us (2%)
    pallas_call x1, Pallas kernels, per_device(): pl.pallas_call(functools.partial(kernel, nd, ns), out_shape=results, in_s...  31.3 us

profile of v4, /device:TPU:1, one launch (start us, length us, event | category | flops | bytes accessed | tf_op | source)
XLA Modules:
  0.0 32.5 jit_solution(1091404376941693660)
XLA Ops:
  0.6 31.3 %trial_energy.1 = (f32[3,4,256]{2,1,0:T(4,128)S(1)}, f32[4]{0:T(128)S(1)}, f32[4]{0:T(128)S(1)}) custom-call(f32[3,256]{1,0:T(4,128)} %coords.1, f32[3,256]{1,0:T(4,128)} %direction.1, s32[4,1024]{1,0:T(4,128)} %connect.1, f32[9,1024]{1,0:T(8,128)} %shape_inv.1, f32[8,128]{1,0:T(8,128)} %bitcast.2, s32[1,128]{1,0:T(1,128)} %send_node.1, s32[1,128]{1,0:T(1,128)} %recv_slot.1), custom_call_target="tpu_custom_call" | custom-call | tf_op jit(solution)/shard_map/trial_energy/pallas_call | solution.py:443
  31.9 0.6 %copy_out.1 = (f32[3,4,256]{2,1,0:T(4,128)}, f32[4]{0:T(128)}, f32[4]{0:T(128)}) custom-call(f32[3,4,256]{2,1,0:T(4,128)S(1)} %get-tuple-element.9.refs_0_, f32[4]{0:T(128)S(1)} %get-tuple-element.10.refs_1_, f32[4]{0:T(128)S(1)} %get-tuple-element.11.refs_2_), custom_call_target="tpu_custom_call" | custom-call | tf_op jit(solution)/shard_map/copy_out/pallas_call | solution.py:481

commit v5 on v4

--- a/solution.py
+++ b/solution.py
@@ -66,22 +66,11 @@
     pltpu.make_async_copy(like, like, sem).wait()
 
 
-def pack(values, op):
+def pack(values, reduce):
     lane = lax.broadcasted_iota(jnp.int32, (8, LANES), 1)
-    half = [op(v, pltpu.roll(v, 64, 1)) for v in values]
-    first = jnp.where(lane < 64, half[0], half[1])
-    second = jnp.where(lane < 64, half[2], half[3])
-    first = op(first, pltpu.roll(first, 32, 1))
-    second = op(second, pltpu.roll(second, 96, 1))
-    return jnp.where((lane // 32) % 2 == 1, first, second)
-
-
-def unpack_mask():
-    lane = lax.broadcasted_iota(jnp.int32, (8, LANES), 1)
-    row = lax.broadcasted_iota(jnp.int32, (8, LANES), 0)
-    group = lane // 32
-    trial = jnp.where(group == 0, 2, jnp.where(group == 1, 0, jnp.where(group == 2, 3, 1)))
-    return trial == row
+    columns = [reduce(v, axis=1, keepdims=True) for v in values]
+    both = jnp.where(lane == 0, columns[0], jnp.where(lane == 1, columns[1], jnp.where(lane == 2, columns[2], columns[3])))
+    return reduce(both, axis=0, keepdims=True)
 
 
 def kernel(
@@ -309,7 +298,7 @@
 
         lax.fori_loop(first, last, step, 0)
 
-    row = jnp.min(pack(dets, jnp.minimum), axis=0, keepdims=True)
+    row = pack(dets, jnp.min)
     rows_v[0] = row
     start_stage(rows_v.at[0], dom_min, dom_sems.at[0], "dom")
     weights = w_v[...]
@@ -332,22 +321,21 @@
     build_hot(chunks // 2, chunks)
     row = finish_stage(row, sub_min, sub_sems.at[0], "sub", jnp.min)
 
-    mask = unpack_mask()
-    lowest = jnp.min(jnp.where(mask, jnp.broadcast_to(row, (8, LANES)), jnp.inf), axis=1, keepdims=True)
+    lowest = row
     shift = lowest - 1.0 - jnp.abs(lowest)
 
     energies = []
     scale_jac = []
     scale_cof = []
     for t in range(TRIALS):
-        lifted = dets[t] - jnp.broadcast_to(shift[t : t + 1, :], (8, LANES))
+        lifted = dets[t] - jnp.broadcast_to(shift[:, t : t + 1], (8, LANES))
         power = jnp.exp(jnp.log(lifted) * (-2.0 / 3.0))
         energy = squares[t] * power
         energies.append(energy)
         scale_jac.append(weights * power * (2.0 / 3.0))
         scale_cof.append(energy / lifted * (2.0 / 9.0))
 
-    row = jnp.sum(pack(energies, jnp.add), axis=0, keepdims=True)
+    row = pack(energies, jnp.sum)
     rows_v[2] = row
     start_stage(rows_v.at[2], sub_sum, sub_sems.at[1], "sub")
 
@@ -394,13 +382,7 @@
     for r in range(3):
         grad_ref[r] = total[TRIALS * r : TRIALS * r + TRIALS, :]
 
-    diagonal = lane == lax.broadcasted_iota(jnp.int32, (8, LANES), 0)
-
-    def along_lanes(column):
-        return jnp.sum(jnp.where(diagonal, column, 0.0), axis=0, keepdims=True)
-
-    finite = jnp.where(lax.broadcasted_iota(jnp.int32, (8, 1), 0) < TRIALS, lowest, 0.0)
-    lowest_ref[...] = along_lanes(finite)[0, :TRIALS]
+    lowest_ref[...] = lowest[0, :TRIALS]
     wait_all(halo, halo_sems.at[0])
     wait_all(gback, back_sems.at[0])
     for i in range(2):
@@ -408,9 +390,8 @@
         wait_all(dom_min.at[pl.ds(0, nd - 1), :], dom_sems.at[i, 0])
 
     row = finish_stage(row, dom_sum, dom_sems.at[1], "dom", jnp.sum)
-    energy = jnp.sum(jnp.where(mask, jnp.broadcast_to(row, (8, LANES)), 0.0), axis=1, keepdims=True)
-    energy = energy / 3.0 / (nd * ns * chunks // 4 * LANES)
-    energy_ref[...] = along_lanes(energy)[0, :TRIALS]
+    energy = row / 3.0 / (nd * ns * chunks // 4 * LANES)
+    energy_ref[...] = energy[0, :TRIALS]
 
 
 def copy_out(*refs):

time: 32.7 us -> 32.4 us (level)
  no operation moved by 1% of the time
where the time goes in v5:
time: 32.4 us; the launch traced here: 32.3 us
  Pallas kernels  31.7 us (98%)
  between operations  0.64 us (2%)
    pallas_call x1, Pallas kernels, per_device(): pl.pallas_call(functools.partial(kernel, nd, ns), out_shape=results, in_s...  31.1 us

profile of v5, /device:TPU:1, one launch (start us, length us, event | category | flops | bytes accessed | tf_op | source)
XLA Modules:
  0.0 32.3 jit_solution(11945158342847556690)
XLA Ops:
  0.6 31.1 %trial_energy.1 = (f32[3,4,256]{2,1,0:T(4,128)S(1)}, f32[4]{0:T(128)S(1)}, f32[4]{0:T(128)S(1)}) custom-call(f32[3,256]{1,0:T(4,128)} %coords.1, f32[3,256]{1,0:T(4,128)} %direction.1, s32[4,1024]{1,0:T(4,128)} %connect.1, f32[9,1024]{1,0:T(8,128)} %shape_inv.1, f32[8,128]{1,0:T(8,128)} %bitcast.2, s32[1,128]{1,0:T(1,128)} %send_node.1, s32[1,128]{1,0:T(1,128)} %recv_slot.1), custom_call_target="tpu_custom_call" | custom-call | tf_op jit(solution)/shard_map/trial_energy/pallas_call | solution.py:424
  31.7 0.6 %copy_out.1 = (f32[3,4,256]{2,1,0:T(4,128)}, f32[4]{0:T(128)}, f32[4]{0:T(128)}) custom-call(f32[3,4,256]{2,1,0:T(4,128)S(1)} %get-tuple-element.9.refs_0_, f32[4]{0:T(128)S(1)} %get-tuple-element.10.refs_1_, f32[4]{0:T(128)S(1)} %get-tuple-element.11.refs_2_), custom_call_target="tpu_custom_call" | custom-call | tf_op jit(solution)/shard_map/copy_out/pallas_call | solution.py:462
